TPU v7x, 128 devices: a whole 4x4x4 slice. The times are simulated.
128 devices in a mesh: teacher: 4 (over y_hi, core), seq: 32 (over x, y_lo, z).
Axes of the slice: x: 4, y: 4 (y_hi: 2, y_lo: 2; y = y_hi * 2 + y_lo), z: 4, core: 2. Of those that a mesh axis runs over, the one named last changes fastest.
Arguments:
- activations: bfloat16 [20, 2048, 1536], P('teacher', 'seq'), may hold values from -150 to 150
- teacher_maps: bfloat16 [4, 20, 2048, 1536], P('teacher', None, 'seq'), may hold values from -6 to 6
- projection: bfloat16 [4, 1536, 1536], P('teacher', 'seq'), may hold values from -0.625 to 0.625
- dilated_weight: bfloat16 [1536, 3, 768], P('seq'), may hold values from -0.09375 to 0.09375
- pointwise_weight: bfloat16 [768, 1536], P('seq'), may hold values from -0.21875 to 0.21875
Outputs:
- loss_mean: float32 [], replicated
- dilated_grad: float32 [1536, 3, 768], P('seq')
- pointwise_grad: float32 [768, 1536], P('seq')
All inputs are finite; a program needn't handle non-finite values.
Results may differ from a plain program's by a relative error of at most 0.00081.
Values may be sent and summed in bfloat16 or wider, within the bound.
No kernel may reach another device: no remote copies, remote signals or barrier semaphores. Data moves between devices by JAX's collectives and lax.ppermute only.
A program may use at most 128 MiB of HBM per device.

v0:
```python
import jax
import jax.numpy as jnp
from jax import lax
from jax.sharding import PartitionSpec as P

TAP_DILATION = 16
slope_const = 0.7978845608
cubic_const = 0.044715


def padded(block, sides, width):
    for axis, dim in sides:
        count = lax.axis_size(axis)
        forward = [(i, i + 1) for i in range(count - 1)]
        backward = [(target, source) for source, target in forward]
        low = lax.ppermute(
            lax.slice_in_dim(block, block.shape[dim] - width, None, axis=dim), axis, forward
        )
        high = lax.ppermute(lax.slice_in_dim(block, 0, width, axis=dim), axis, backward)
        block = jnp.concatenate([low, block, high], axis=dim)
    return block


def gelu_tanh(value):
    inside = slope_const * (value + cubic_const * value * value * value)
    return 0.5 * value * (1.0 + jnp.tanh(inside))


def gelu_slope(value):
    inside = slope_const * (value + cubic_const * value * value * value)
    tangent = jnp.tanh(inside)
    return 0.5 * (1.0 + tangent) + 0.5 * value * (1.0 - tangent * tangent) * slope_const * (
        1.0 + 3.0 * cubic_const * value * value
    )


def column_product(left, right):
    return lax.dot_general(
        left, right, (((0,), (0,)), ((), ())), preferred_element_type=jnp.float32
    )


def shards(activations, teacher_maps, projection, dilated_weight, pointwise_weight):
    groups = lax.axis_size("teacher")
    ranks = lax.axis_size("seq")
    win_grp, bins_per_device, channel_count = activations.shape
    branch_width = dilated_weight.shape[2]
    count_of_rows = win_grp * bins_per_device
    total_rows = count_of_rows * groups * ranks
    maps_flat = teacher_maps[0].reshape(-1, teacher_maps.shape[3])
    columns = maps_flat
    projected = jnp.dot(
        columns,
        lax.all_gather(projection, "seq", axis=1, tiled=True)[0],
        preferred_element_type=jnp.float32,
    )
    projected = lax.optimization_barrier(projected.astype(jnp.bfloat16)).astype(jnp.float32)
    summed = lax.psum(projected, "teacher")
    own_rows = lax.dynamic_slice_in_dim(
        summed, lax.axis_index("teacher") * count_of_rows, count_of_rows, 0
    )
    target = own_rows / groups
    inputs_f = activations.reshape(count_of_rows, channel_count).astype(jnp.float32)
    sum_first, sum_second = lax.psum(
        (jnp.sum(inputs_f, axis=0), jnp.sum(inputs_f * inputs_f, axis=0)), ("teacher", "seq")
    )
    channel_mean = sum_first / total_rows
    channel_var = sum_second / total_rows - channel_mean * channel_mean
    normed = (inputs_f - channel_mean) * lax.rsqrt(channel_var + 1e-05)
    hidden_state = (
        gelu_tanh(normed).astype(jnp.bfloat16).reshape(win_grp, bins_per_device, channel_count)
    )
    padded_input = padded(hidden_state, (("seq", 1),), TAP_DILATION)
    tap_weights = [
        padded_input[
            :, offset_index * TAP_DILATION : offset_index * TAP_DILATION + bins_per_device
        ].reshape(count_of_rows, channel_count)
        for offset_index in range(3)
    ]
    running = jnp.zeros((count_of_rows, branch_width), jnp.float32)
    section = lax.all_gather(dilated_weight, "seq", axis=0, tiled=True)
    for offset_index in range(3):
        columns = tap_weights[offset_index]
        running = running + jnp.dot(
            columns, section[:, offset_index, :], preferred_element_type=jnp.float32
        )
    activated = gelu_tanh(running).astype(jnp.bfloat16)
    pointwise_full = lax.all_gather(pointwise_weight, "seq", axis=0, tiled=True)
    student = inputs_f + jnp.dot(activated, pointwise_full, preferred_element_type=jnp.float32)
    misfit = student - target
    squared_total = lax.psum(jnp.sum(misfit * misfit), ("teacher", "seq"))
    loss_mean = 0.5 * squared_total / (channel_count * total_rows)
    out_grad = (misfit / channel_count).astype(jnp.bfloat16)
    back_grad = lax.dot_general(
        out_grad, pointwise_full, (((1,), (1,)), ((), ())), preferred_element_type=jnp.float32
    )
    preact_grad = (back_grad * gelu_slope(running)).astype(jnp.bfloat16)
    dilated_part = lax.psum_scatter(
        jnp.stack(
            [column_product(tap_weights[offset_index], preact_grad) for offset_index in range(3)],
            axis=1,
        ),
        "seq",
        scatter_dimension=0,
        tiled=True,
    )
    pointwise_part = lax.psum_scatter(
        column_product(activated, out_grad), "seq", scatter_dimension=0, tiled=True
    )
    dilated_grad, pointwise_grad = lax.psum((dilated_part, pointwise_part), "teacher")
    return (loss_mean, dilated_grad, pointwise_grad)


def solution(mesh):
    in_specs = (
        P("teacher", "seq", None),
        P("teacher", None, "seq", None),
        P("teacher", "seq", None),
        P("seq", None, None),
        P("seq", None),
    )
    out_specs = (P(), P("seq", None, None), P("seq", None))
    return jax.shard_map(shards, mesh=mesh, in_specs=in_specs, out_specs=out_specs, check_vma=False)
```

profile of v0, /device:TPU:1, one launch (start us, length us, event | category | flops | bytes accessed | tf_op | source)
XLA Modules:
  0.0 940.9 jit_solution(16138648876742079881)
XLA Ops:
  7.2 0.7 all-gather.8.cloned.1.call-update
  8.0 0.7 all-gather.4.cloned.1.call-update
  8.7 1.5 convert_reduce_fusion
  10.2 71.5 %all-reduce = (f32[1536]{0:T(1024)S(1)}, f32[1536]{0:T(1024)S(1)}) all-reduce(f32[1536]{0:T(1024)S(1)} %get-tuple-element.4, f32[1536]{0:T(1024)S(1)} %get-tuple-element.3), channel_id=1, replica_groups=mesh['teacher'=4,'seq'=32] {'teacher','seq'}, use_global_device_ids=true, to_apply=%region_3.0 | all-reduce | flops 3072 | bytes 24576 | tf_op jit(solution)/shard_map/psum | solution.py:64
  81.7 0.8 fusion.9
  82.6 1.3 collective-permute-start
  83.9 1.3 collective-permute-start.1
  85.3 5.7 collective-permute-done
  91.0 4.3 collective-permute-done.1
  95.2 1.2 pad_maximum_fusion.2
  96.4 54.6 %all-gather.8.cloned.1.call-done = bf16[1,1536,1536]{2,1,0:T(8,128)(2,1)} async-done(((bf16[1,48,1536]{2,1,0:T(8,128)(2,1)}), bf16[1,1536,1536]{2,1,0:T(8,128)(2,1)}) %all-gather.8.cloned.1.call-update) | async-done | bytes 4718608 | tf_op jit(solution)/shard_map/all_gather | solution.py:54
  151.0 10.7 %convolution_convert_fusion = bf16[1280,1536]{1,0:T(8,128)(2,1)} fusion(bf16[1280,1536]{1,0:T(8,128)(2,1)} %bitcast.55, bf16[1,1536,1536]{2,1,0:T(8,128)(2,1)} %all-gather.8.cloned.1.call-done), kind=kOutput, calls=%fused_computation.1 | convolution fusion | flops 6041763840 | bytes 12582912 | tf_op jit(solution)/shard_map/dot_general | solution.py:52
  161.7 239.2 %all-reduce.6 = f32[1280,1536]{1,0:T(8,128)} all-reduce(bf16[1280,1536]{1,0:T(8,128)(2,1)} %convolution_convert_fusion), channel_id=1, replica_groups=mesh['teacher'=4,'seq'=32] {'teacher'}, use_global_device_ids=true, to_apply=%region_4.0 | all-reduce | flops 1966080 | bytes 11796480 | tf_op jit(solution)/shard_map/psum | solution.py:58
  400.9 2.7 fusion.3
  403.6 2.6 fusion.2
  406.2 3.6 fusion.21
  409.8 60.0 %all-gather.6.cloned.1.call-done = bf16[768,1536]{1,0:T(8,128)(2,1)} async-done(((bf16[24,1536]{1,0:T(8,128)(2,1)}), bf16[768,1536]{1,0:T(8,128)(2,1)}) %all-gather.6.cloned.1.call-update) | async-done | bytes 2359312 | tf_op jit(solution)/shard_map/all_gather | solution.py:88
  469.8 4.4 multiply_reduce_fusion
  474.2 3.7 fusion.28
  478.0 0.2 reduce-scatter.3.cloned.1.call-start
  478.2 0.8 fusion.14
  479.0 0.4 copy-done.2
  479.4 3.0 fusion.22
  482.4 3.6 convolution_bitcast_fusion
  486.0 3.6 convolution_bitcast_fusion.2
  489.6 3.7 convolution_bitcast_fusion.1
  493.3 11.1 %pad_maximum_fusion = f32[1536,3,768]{2,0,1:T(8,128)} fusion(f32[1536,1,768]{2,0,1:T(8,128)} %convolution_bitcast_fusion, f32[1536,1,768]{2,0,1:T(8,128)} %convolution_bitcast_fusion.1, f32[1536,1,768]{2,0,1:T(8,128)} %convolution_bitcast_fusion.2), kind=kLoop, calls=%fused_computation | loop fusion | flops 7077888 | bytes 28311552 | tf_op jit(solution)/shard_map/stack | solution.py:99
  504.4 145.1 %reduce-scatter.5.cloned.1.call-done = f32[24,1536]{1,0:T(8,128)} async-done(((f32[768,1536]{1,0:T(8,128)}), f32[24,1536]{1,0:T(8,128)}) %reduce-scatter.5.cloned.1.call-update) | async-done | bytes 147472 | tf_op jit(solution)/shard_map/reduce_scatter | solution.py:107
  649.5 194.7 %reduce-scatter.3.cloned.1.call-done = f32[48,3,768]{2,0,1:T(8,128)} async-done(((f32[1536,3,768]{2,0,1:T(8,128)}), f32[48,3,768]{2,0,1:T(8,128)}) %reduce-scatter.3.cloned.1.call-update) | async-done | bytes 442384 | tf_op jit(solution)/shard_map/reduce_scatter | solution.py:98
  844.2 84.7 %psum.45 = f32[]{:T(128)} all-reduce(f32[]{:T(128)} %get-tuple-element.15), channel_id=1, replica_groups=mesh['teacher'=4,'seq'=32] {'teacher','seq'}, use_global_device_ids=true, to_apply=%region_6.0 | all-reduce | flops 1 | bytes 8 | tf_op jit(solution)/shard_map/psum | solution.py:91
  929.6 1.8 copy.12
  931.4 1.6 copy.13
  (26 shorter events, 0.4 us)
Async XLA Ops:
  7.2 74.5 %copy-start = (bf16[5,64,1536]{2,1,0:T(8,128)(2,1)S(1)}, bf16[5,64,1536]{2,1,0:T(8,128)(2,1)}, u32[]{:S(2)}) copy-start(bf16[5,64,1536]{2,1,0:T(8,128)(2,1)} %param.5) | copy-start | bytes 2949124
  7.2 143.8 %all-gather.8.cloned.1.call-start = ((), (), s32[]{:S(2)}) async-start(), calls=%async_computation.4 | async-start | bytes 4866048 | tf_op jit(solution)/shard_map/all_gather | solution.py:54
  7.9 393.0 %all-gather.4.cloned.1.call-start = ((), (), s32[]{:S(2)}) async-start(), calls=%async_computation.2 | async-start | bytes 7299072 | tf_op jit(solution)/shard_map/all_gather | solution.py:81
  8.7 461.1 %all-gather.6.cloned.1.call-start = ((), (), s32[]{:S(2)}) async-start(), calls=%async_computation.3 | async-start | bytes 2433024 | tf_op jit(solution)/shard_map/all_gather | solution.py:88
  82.6 8.4 collective-permute-start
  83.9 11.4 %collective-permute-start.1 = (bf16[5,16,1536]{2,1,0:T(8,128)(2,1)S(1)}, bf16[5,16,1536]{2,1,0:T(8,128)(2,1)S(1)}, u32[]{:S(2)}, u32[]{:S(2)}) collective-permute-start(bf16[5,16,1536]{2,1,0:T(8,128)(2,1)S(1)} %get-tuple-element.12), channel_id=1, source_target_pairs={{1,0},{2,1},{3,2},{4,3},{5,4},{6,5},{7,6},{8,7},{9,8},{10,9},{11,1... | collective-permute-start | bytes 737288 | tf_op jit(solution)/shard_map/ppermute | solution.py:19
  85.2 564.3 %reduce-scatter.5.cloned.1.call-start = ((), (), s32[]{:S(2)}) async-start(), calls=%async_computation.6 | async-start | bytes 4866048 | tf_op jit(solution)/shard_map/reduce_scatter | solution.py:107
  96.4 309.8 %copy-start.3 = (bf16[5,64,1536]{2,1,0:T(8,128)(2,1)}, bf16[5,64,1536]{2,1,0:T(8,128)(2,1)S(1)}, u32[]{:S(2)}) copy-start(bf16[5,64,1536]{2,1,0:T(8,128)(2,1)S(1)} %get-tuple-element.9) | copy-start | bytes 2949124
  400.9 2.7 copy-start.5
  469.8 4.4 copy-start.1
  478.0 366.2 %reduce-scatter.3.cloned.1.call-start = ((), (), s32[]{:S(2)}) async-start(), calls=%async_computation.5 | async-start | bytes 14598144 | tf_op jit(solution)/shard_map/reduce_scatter | solution.py:98
  478.2 1.2 copy-start.2
  479.4 3.0 copy-start.6
  482.4 3.6 copy-start.4
  504.3 425.2 %all-reduce.5.cloned.1.call-start = ((), (), s32[]{:S(2)}) async-start(), calls=%async_computation.7 | async-start | bytes 1179648 | tf_op jit(solution)/shard_map/psum | solution.py:110
Sparse Core Ops, SparseCore 0:
  9.6 141.3 all-gather.7
  152.6 172.9 all-gather.3
  327.3 142.4 all-gather.5
  478.1 171.3 reduce-scatter.4
  651.8 192.3 reduce-scatter.2
  846.6 61.8 all-reduce.4
where the time goes:
time: 941 us
  waiting for transfers between devices  466 us (50%)
  blocking collectives  395 us (42%)
  matrix products  41.5 us (4%)
  between operations  16 us (2%)
  other arithmetic  15.3 us (2%)
    psum x1, blocking collectives, shards(): summed = lax.psum(projected, 'teacher')  239 us
    reduce_scatter x1, waiting for transfers between devices, shards(): lax.psum_scatter(jnp.stack([column_product(tap_weights[offset_index], pre...  195 us
    reduce_scatter x1, waiting for transfers between devices, shards(): lax.psum_scatter(column_product(activated, out_grad), 'seq', scatter_dime...  145 us
    psum x1, blocking collectives, shards(): squared_total = lax.psum(jnp.sum(misfit * misfit), ('teacher', 'seq'))  84.7 us
    psum x1, blocking collectives, shards(): lax.psum((jnp.sum(inputs_f, axis=0), jnp.sum(inputs_f * inputs_f, axis=0)...  71.5 us
    all_gather x1, waiting for transfers between devices, shards(): pointwise_full = lax.all_gather(pointwise_weight, 'seq', axis=0, tiled=True)  60 us
    all_gather x1, waiting for transfers between devices, shards(): lax.all_gather(projection, 'seq', axis=1, tiled=True)[0]  54.6 us
  transfers between devices with their start and end apart: 8, of which 6 were waited for; matrix products, arithmetic and copies ran while one was open for 5% of the time, Pallas kernels for 0%

commit v1 on v0

--- a/solution.py
+++ b/solution.py
@@ -55,7 +55,7 @@
         preferred_element_type=jnp.float32,
     )
     projected = lax.optimization_barrier(projected.astype(jnp.bfloat16)).astype(jnp.float32)
-    summed = lax.psum(projected, "teacher")
+    summed = jnp.sum(lax.all_gather(projected, "teacher"), axis=0)
     own_rows = lax.dynamic_slice_in_dim(
         summed, lax.axis_index("teacher") * count_of_rows, count_of_rows, 0
     )

time: 941 us -> 1140 us (1.21)
  waiting for transfers between devices: 466 us -> 864 us
  blocking collectives: 395 us -> 173 us
  other arithmetic: 15.3 us -> 33.8 us
    psum x1 -> x0, blocking collectives: 239 us -> none  [shards(): summed = lax.psum(projected, 'teacher')]
    all_gather x0 -> x1, waiting for transfers between devices: none -> 207 us  [shards(): summed = jnp.sum(lax.all_gather(projected, 'teacher'), axis=0)]
    all_gather x1, waiting for transfers between devices: 54.6 us -> 141 us  [shards(): lax.all_gather(projection, 'seq', axis=1, tiled=True)[0]]
    all_gather x1, waiting for transfers between devices: 60 us -> 117 us  [shards(): pointwise_full = lax.all_gather(pointwise_weight, 'seq', axis=0, tiled=True)]
    all_gather x1, waiting for transfers between devices: 0.01 us -> 44.4 us  [shards(): section = lax.all_gather(dilated_weight, 'seq', axis=0, tiled=True)]
    psum x1, blocking collectives: 71.5 us -> 89.9 us  [shards(): lax.psum((jnp.sum(inputs_f, axis=0), jnp.sum(inputs_f * inputs_f, axis=0)...]
    reduce_sum x0 -> x1, other arithmetic: none -> 15.5 us  [shards(): summed = jnp.sum(lax.all_gather(projected, 'teacher'), axis=0)]
  transfers between devices with their start and end apart: 8 -> 9, of which waited for: 6 -> 8; matrix products, arithmetic and copies ran while one was open for 5% -> 5% of each run, Pallas kernels for 0% -> 0%
where the time goes in v1:
time: 1140 us
  waiting for transfers between devices  864 us (76%)
  blocking collectives  173 us (15%)
  matrix products  40.3 us (4%)
  other arithmetic  33.8 us (3%)
  between operations  16 us (1%)
    all_gather x1, waiting for transfers between devices, shards(): summed = jnp.sum(lax.all_gather(projected, 'teacher'), axis=0)  207 us
    reduce_scatter x1, waiting for transfers between devices, shards(): lax.psum_scatter(jnp.stack([column_product(tap_weights[offset_index], pre...  197 us
    reduce_scatter x1, waiting for transfers between devices, shards(): lax.psum_scatter(column_product(activated, out_grad), 'seq', scatter_dime...  144 us
    all_gather x1, waiting for transfers between devices, shards(): lax.all_gather(projection, 'seq', axis=1, tiled=True)[0]  141 us
    all_gather x1, waiting for transfers between devices, shards(): pointwise_full = lax.all_gather(pointwise_weight, 'seq', axis=0, tiled=True)  117 us
    psum x1, blocking collectives, shards(): lax.psum((jnp.sum(inputs_f, axis=0), jnp.sum(inputs_f * inputs_f, axis=0)...  89.9 us
    psum x1, blocking collectives, shards(): squared_total = lax.psum(jnp.sum(misfit * misfit), ('teacher', 'seq'))  83.4 us
    all_gather x1, waiting for transfers between devices, shards(): section = lax.all_gather(dilated_weight, 'seq', axis=0, tiled=True)  44.4 us
  transfers between devices with their start and end apart: 9, of which 8 were waited for; matrix products, arithmetic and copies ran while one was open for 5% of the time, Pallas kernels for 0%

profile of v1, /device:TPU:1, one launch (start us, length us, event | category | flops | bytes accessed | tf_op | source)
XLA Modules:
  0.0 1135.7 jit_solution(12413517175812367093)
XLA Ops:
  7.2 0.7 all-gather.10.cloned.1.call-update
  7.9 0.7 all-gather.6.cloned.1.call-update
  8.7 141.5 %all-gather.10.cloned.1.call-done = bf16[1,1536,1536]{2,1,0:T(8,128)(2,1)} async-done(((bf16[1,48,1536]{2,1,0:T(8,128)(2,1)}), bf16[1,1536,1536]{2,1,0:T(8,128)(2,1)}) %all-gather.10.cloned.1.call-update) | async-done | bytes 4718608 | tf_op jit(solution)/shard_map/all_gather | solution.py:54
  150.1 9.3 convolution_convert_fusion
  159.5 4.2 all_gather.24
  165.2 89.9 %all-reduce = (f32[1536]{0:T(1024)S(1)}, f32[1536]{0:T(1024)S(1)}) all-reduce(f32[1536]{0:T(1024)S(1)} %get-tuple-element.4, f32[1536]{0:T(1024)S(1)} %get-tuple-element.3), channel_id=1, replica_groups=mesh['teacher'=4,'seq'=32] {'teacher','seq'}, use_global_device_ids=true, to_apply=%region_3.0 | all-reduce | flops 3072 | bytes 24576 | tf_op jit(solution)/shard_map/psum | solution.py:64
  255.1 0.8 fusion.9
  256.0 2.3 collective-permute-start
  258.3 1.3 collective-permute-start.1
  259.6 6.9 collective-permute-done
  266.5 4.3 collective-permute-done.1
  270.8 1.1 pad_maximum_fusion.2
  272.0 44.4 %all-gather.6.cloned.1.call-done = bf16[1536,3,768]{2,0,1:T(8,128)(2,1)} async-done(((bf16[48,3,768]{2,0,1:T(8,128)(2,1)}), bf16[1536,3,768]{2,0,1:T(8,128)(2,1)}) %all-gather.6.cloned.1.call-update) | async-done | bytes 7077904 | tf_op jit(solution)/shard_map/all_gather | solution.py:81
  316.3 2.9 fusion.2
  319.2 2.6 fusion.3
  321.8 3.6 fusion.21
  325.4 207.0 %all-gather.12.cloned.1.call-done = f32[5120,1536]{1,0:T(8,128)} async-done(((f32[1280,1536]{1,0:T(8,128)}), f32[5120,1536]{1,0:T(8,128)}) %all-gather.12.cloned.1.call-update) | async-done | bytes 31457296 | tf_op jit(solution)/shard_map/all_gather | solution.py:58
  532.4 15.5 %reduce_sum.38 = f32[1280,1536]{1,0:T(8,128)} reduce(f32[4,1280,1536]{2,1,0:T(8,128)} %bitcast.50, f32[]{:T(128)} %constant.16.clone.1), dimensions={0}, to_apply=%region_4.0 | reduce | flops 5898240 | bytes 39321604 | tf_op jit(solution)/shard_map/reduce_sum | solution.py:58
  547.9 116.8 %all-gather.8.cloned.1.call-done = bf16[768,1536]{1,0:T(8,128)(2,1)} async-done(((bf16[24,1536]{1,0:T(8,128)(2,1)}), bf16[768,1536]{1,0:T(8,128)(2,1)}) %all-gather.8.cloned.1.call-update) | async-done | bytes 2359312 | tf_op jit(solution)/shard_map/all_gather | solution.py:88
  664.7 4.4 multiply_reduce_fusion
  669.1 3.7 fusion.28
  673.1 0.8 fusion.14
  674.3 3.0 fusion.22
  677.4 3.6 convolution_bitcast_fusion
  681.0 3.5 convolution_bitcast_fusion.2
  684.5 3.6 convolution_bitcast_fusion.1
  688.2 11.1 pad_maximum_fusion
  699.3 144.0 %reduce-scatter.5.cloned.1.call-done = f32[24,1536]{1,0:T(8,128)} async-done(((f32[768,1536]{1,0:T(8,128)}), f32[24,1536]{1,0:T(8,128)}) %reduce-scatter.5.cloned.1.call-update) | async-done | bytes 147472 | tf_op jit(solution)/shard_map/reduce_scatter | solution.py:107
  843.3 196.9 %reduce-scatter.3.cloned.1.call-done = f32[48,3,768]{2,0,1:T(8,128)} async-done(((f32[1536,3,768]{2,0,1:T(8,128)}), f32[48,3,768]{2,0,1:T(8,128)}) %reduce-scatter.3.cloned.1.call-update) | async-done | bytes 442384 | tf_op jit(solution)/shard_map/reduce_scatter | solution.py:98
  1040.2 83.4 %psum.37 = f32[]{:T(128)} all-reduce(f32[]{:T(128)} %get-tuple-element.15), channel_id=1, replica_groups=mesh['teacher'=4,'seq'=32] {'teacher','seq'}, use_global_device_ids=true, to_apply=%region_6.0 | all-reduce | flops 1 | bytes 8 | tf_op jit(solution)/shard_map/psum | solution.py:91
  1124.3 1.8 copy.10
  1126.1 1.6 copy.11
  (28 shorter events, 2.3 us)
Async XLA Ops:
  7.2 143.0 %all-gather.10.cloned.1.call-start = ((), (), s32[]{:S(2)}) async-start(), calls=%async_computation.4 | async-start | bytes 4866048 | tf_op jit(solution)/shard_map/all_gather | solution.py:54
  7.9 308.4 %all-gather.6.cloned.1.call-start = ((), (), s32[]{:S(2)}) async-start(), calls=%async_computation.2 | async-start | bytes 7299072 | tf_op jit(solution)/shard_map/all_gather | solution.py:81
  8.6 523.8 %all-gather.12.cloned.1.call-start = ((), (), s32[]{:S(2)}) async-start(), calls=%async_computation.7 | async-start | bytes 39321600 | tf_op jit(solution)/shard_map/all_gather | solution.py:58
  163.7 1.2 copy-start
  163.7 501.0 %all-gather.8.cloned.1.call-start = ((), (), s32[]{:S(2)}) async-start(), calls=%async_computation.3 | async-start | bytes 2433024 | tf_op jit(solution)/shard_map/all_gather | solution.py:88
  164.3 679.0 %reduce-scatter.5.cloned.1.call-start = ((), (), s32[]{:S(2)}) async-start(), calls=%async_computation.6 | async-start | bytes 4866048 | tf_op jit(solution)/shard_map/reduce_scatter | solution.py:107
  256.0 10.5 collective-permute-start
  258.3 12.6 %collective-permute-start.1 = (bf16[5,16,1536]{2,1,0:T(8,128)(2,1)S(1)}, bf16[5,16,1536]{2,1,0:T(8,128)(2,1)S(1)}, u32[]{:S(2)}, u32[]{:S(2)}) collective-permute-start(bf16[5,16,1536]{2,1,0:T(8,128)(2,1)S(1)} %get-tuple-element.12), channel_id=1, source_target_pairs={{1,0},{2,1},{3,2},{4,3},{5,4},{6,5},{7,6},{8,7},{9,8},{10,9},{11,1... | collective-permute-start | bytes 737288 | tf_op jit(solution)/shard_map/ppermute | solution.py:19
  272.0 49.9 %copy-start.3 = (bf16[5,64,1536]{2,1,0:T(8,128)(2,1)}, bf16[5,64,1536]{2,1,0:T(8,128)(2,1)S(1)}, u32[]{:S(2)}) copy-start(bf16[5,64,1536]{2,1,0:T(8,128)(2,1)S(1)} %get-tuple-element.9) | copy-start | bytes 2949124
  664.7 4.4 copy-start.1
  672.9 367.4 %reduce-scatter.3.cloned.1.call-start = ((), (), s32[]{:S(2)}) async-start(), calls=%async_computation.5 | async-start | bytes 14598144 | tf_op jit(solution)/shard_map/reduce_scatter | solution.py:98
  673.1 1.2 copy-start.2
  674.3 3.0 copy-start.5
  677.3 3.6 copy-start.4
  699.2 425.0 %all-reduce.4.cloned.1.call-start = ((), (), s32[]{:S(2)}) async-start(), calls=%async_computation.8 | async-start | bytes 1179648 | tf_op jit(solution)/shard_map/psum | solution.py:110
Sparse Core Ops, SparseCore 0:
  9.6 140.4 all-gather.9
  151.8 164.4 all-gather.5
  318.0 214.3 all-gather.11
  533.9 130.7 all-gather.7
  673.0 170.2 reduce-scatter.4
  845.6 194.5 reduce-scatter.2
  1042.8 60.5 all-reduce.3
